TPU v7x, 32 devices: a whole 2x2x4 slice. The times are simulated.
32 devices in a mesh: row: 2 (over x), col: 16 (over z, y, core).
Axes of the slice: x: 2, y: 2, z: 4, core: 2. Of those that a mesh axis runs over, the one named last changes fastest.
Arguments:
- src_pos: float32 [3, 8192], P(None, 'row'), may hold values from 0 to 1
- src_desc: bfloat16 [64, 8192], P(None, 'row'), may hold values from -2.5 to 2.5
- src_mass: float32 [8192], P('row'), may hold values from 0.2 to 5
- tgt_pos: float32 [3, 8192], P(None, 'col'), may hold values from 0 to 1
- tgt_desc: bfloat16 [64, 8192], P(None, 'col'), may hold values from -2.5 to 2.5
- tgt_mass: float32 [8192], P('col'), may hold values from 0.2 to 5
- pattern: int32 [64, 20], P('row'), may hold values from 0 to 63, all different within a row
Outputs:
- row_potential: float32 [8192], P('row')
- col_potential: float32 [8192], P('col')
- mapped_desc: float32 [8192, 64], P(('row', 'col'))
Inputs may be any that keep to these rules, and one draw needn't show every extreme that they name: `pattern`: each row names 20 different target clusters, and every target cluster is named by some row.
All inputs are finite; a program needn't handle non-finite values.
Results may differ from a plain program's by a relative error of at most 0.0028.
Values may be sent and summed in bfloat16 or wider, within the bound.
A program may use at most 64 MiB of HBM per device.

v0:
```python
import functools
import math

import jax
import jax.numpy as jnp
from jax import lax
from jax.experimental import pallas as pl
from jax.experimental.pallas import tpu as pltpu
from jax.sharding import PartitionSpec as P

CL = 128
EPSILON = 0.05
LOG2E = 1.0 / math.log(2.0)
SCORE_SCALE = 2.0 * LOG2E / EPSILON
POT_SCALE = EPSILON * math.log(2.0)
MASKED = -(2.0**93)
MESH = pl.DeviceIdType.MESH
NUM_ROWS = 16


def log2(value):
    return jnp.log(value) * LOG2E


def float_parts(value):
    first = value.astype(jnp.bfloat16).astype(jnp.float32)
    rest = value - first
    second = rest.astype(jnp.bfloat16).astype(jnp.float32)
    return first, second, (rest - second).astype(jnp.bfloat16).astype(jnp.float32)


def hi_lo(value):
    high = value.astype(jnp.bfloat16)
    low = (value - high.astype(jnp.float32)).astype(jnp.bfloat16)
    return high, low


def hi_lo_rows(value):
    high = value.astype(jnp.bfloat16).astype(jnp.float32)
    low = value - high
    row = lax.broadcasted_iota(jnp.int32, (NUM_ROWS, value.shape[1]), 0)
    rows = jnp.where(row == 0, high, jnp.where(row == 1, low, 0.0))
    return rows.astype(jnp.bfloat16)


def kernel(
    n_row, n_col,
    src_pos_ref, src_desc_ref, src_mask_ref, src_mass_ref, tgt_pos_ref, desc_ref, tgt_mass_ref,
    row_out, col_out, map_out,
    src_feat, tgt_feat, score, plan, stat_send, stat_recv, rp_all, col_max, col_sum, col_stat, sum_send, sum_recv, u_all,
    col_part, num_send, num_recv,
    stat_ss, stat_rs, rp_ss, rp_rs, cs_ss, cs_rs, sum_ss, sum_rs, u_ss, u_rs, cp_ss, cp_rs, num_ss, num_rs,
):
    me = lax.axis_index("col")
    mine = lax.axis_index("row")
    n_tgt = desc_ref.shape[1]
    width = map_out.shape[1]
    fold = min(width, 128)
    n_feat = desc_ref.shape[0]

    def col_peer(offset):
        return lax.rem(me + offset, n_col)

    def row_peer(offset):
        return lax.rem(mine + offset, n_row)

    barrier = pltpu.get_barrier_semaphore()

    @pl.loop(1, n_col)
    def _(offset):
        pl.semaphore_signal(barrier, inc=1, device_id={"col": col_peer(offset)}, device_id_type=MESH)

    @pl.loop(1, n_row)
    def _(offset):
        pl.semaphore_signal(barrier, inc=1, device_id={"row": row_peer(offset)}, device_id_type=MESH)

    def to_owner(send, recv, ssem, rsem, peer):
        return pltpu.make_async_remote_copy(
            src_ref=send.at[peer], dst_ref=recv.at[me], send_sem=ssem.at[peer], recv_sem=rsem.at[me],
            device_id={"col": peer}, device_id_type=MESH,
        )

    def from_peer(send, recv, ssem, rsem, peer):
        return pltpu.make_async_remote_copy(
            src_ref=send.at[peer], dst_ref=recv.at[peer], send_sem=ssem.at[peer], recv_sem=rsem.at[peer],
            device_id={"col": peer}, device_id_type=MESH,
        )

    def spread(buf, ssem, rsem, peer):
        return pltpu.make_async_remote_copy(
            src_ref=buf.at[me], dst_ref=buf.at[me], send_sem=ssem.at[peer], recv_sem=rsem.at[me],
            device_id={"col": peer}, device_id_type=MESH,
        )

    def spread_from(buf, ssem, rsem, peer):
        return pltpu.make_async_remote_copy(
            src_ref=buf.at[me], dst_ref=buf.at[peer], send_sem=ssem.at[peer], recv_sem=rsem.at[peer],
            device_id={"col": peer}, device_id_type=MESH,
        )

    def row_spread(buf, ssem, rsem, peer):
        return pltpu.make_async_remote_copy(
            src_ref=buf.at[mine], dst_ref=buf.at[mine], send_sem=ssem.at[peer], recv_sem=rsem.at[mine],
            device_id={"row": peer}, device_id_type=MESH,
        )

    def row_spread_from(buf, ssem, rsem, peer):
        return pltpu.make_async_remote_copy(
            src_ref=buf.at[mine], dst_ref=buf.at[peer], send_sem=ssem.at[peer], recv_sem=rsem.at[peer],
            device_id={"row": peer}, device_id_type=MESH,
        )

    def block_of(ref, block):
        if ref.ndim == 3:
            return ref[block]
        return ref[:, pl.ds(pl.multiple_of(block * width, 128), width)]

    desc32 = desc_ref[...].astype(jnp.float32)
    tgt_pos = tgt_pos_ref[...]
    norm = jnp.sum(tgt_pos * tgt_pos, axis=0, keepdims=True) + jnp.sum(desc32 * desc32, axis=0, keepdims=True)
    n_mask = src_mask_ref.shape[-2]
    lane = lax.broadcasted_iota(jnp.int32, (n_mask, n_tgt), 1) // CL
    in_cluster = lane == lax.broadcasted_iota(jnp.int32, (n_mask, n_tgt), 0)
    t1, t2, t3 = float_parts(jnp.concatenate([tgt_pos, -0.5 * norm, jnp.where(in_cluster, 1.0, 0.0)], axis=0))
    tgt_feat[...] = jnp.concatenate([desc32, t1, t2, t1, t2, t3, t1], axis=0).T.astype(jnp.bfloat16)
    ones = jnp.ones((1, width), jnp.float32)

    def row_stat(block):
        s1, s2, s3 = float_parts(
            jnp.concatenate([block_of(src_pos_ref, block), ones, block_of(src_mask_ref, block)], axis=0)
        )
        src_feat[0:n_feat, :] = block_of(src_desc_ref, block)
        src_feat[n_feat:, :] = jnp.concatenate([s1, s1, s2, s2, s1, s3], axis=0).astype(jnp.bfloat16)
        score[block] = SCORE_SCALE * jnp.dot(
            tgt_feat[...], src_feat[...], preferred_element_type=jnp.float32
        )
        peak = jnp.max(score[block], axis=0, keepdims=True)
        total = jnp.sum(jnp.exp2(score[block] - peak), axis=0, keepdims=True)
        return peak, total

    peak, total = row_stat(me)
    stat_recv[me, 0:1, :] = peak
    stat_recv[me, 1:2, :] = total
    pl.semaphore_wait(barrier, n_col - 1 + n_row - 1)

    @pl.loop(1, n_col)
    def _(offset):
        peer = col_peer(offset)
        peak, total = row_stat(peer)
        stat_send[peer, 0:1, :] = peak
        stat_send[peer, 1:2, :] = total
        to_owner(stat_send, stat_recv, stat_ss, stat_rs, peer).start()

    @pl.loop(1, n_col)
    def _(offset):
        from_peer(stat_send, stat_recv, stat_ss, stat_rs, col_peer(offset)).wait()

    peaks = stat_recv[:, 0:1, :]
    top = jnp.max(peaks, axis=0, keepdims=True)
    row_total = jnp.sum(stat_recv[:, 1:2, :] * jnp.exp2(peaks - top), axis=0)
    own_mass = block_of(src_mass_ref, me)
    rp_all[me] = log2(own_mass) - (top[0] + log2(row_total))

    @pl.loop(1, n_col)
    def _(offset):
        spread(rp_all, rp_ss, rp_rs, col_peer(offset)).start()

    @pl.loop(1, n_col)
    def _(offset):
        spread_from(rp_all, rp_ss, rp_rs, col_peer(offset)).wait()

    strip = 64

    def folded(value, join):
        parts = [value[:, at : at + fold] for at in range(0, width, fold)]
        return functools.reduce(join, parts)

    @pl.loop(0, n_tgt // strip)
    def _(index):
        rows = pl.ds(pl.multiple_of(index * strip, strip), strip)

        def highest(block, running):
            return jnp.maximum(running, folded(score[block, rows, :] + rp_all[block], jnp.maximum))

        running = lax.fori_loop(0, n_col, highest, jnp.full((strip, fold), -3e38, jnp.float32), unroll=4)
        col_max[rows, :] = running
        peak = jnp.max(running, axis=1, keepdims=True)

        def summed(block, running):
            part = jnp.exp2(score[block, rows, :] + (rp_all[block] - peak))
            plan[block, rows, :] = part.astype(jnp.bfloat16)
            return running + folded(part, jnp.add)

        col_sum[rows, :] = lax.fori_loop(0, n_col, summed, jnp.zeros((strip, fold), jnp.float32), unroll=4)

    own_peak = jnp.max(col_max[...].T, axis=0, keepdims=True)
    col_stat[mine, 0:1, :] = own_peak
    col_stat[mine, 1:2, :] = jnp.sum(col_sum[...].T, axis=0, keepdims=True)

    @pl.loop(1, n_row)
    def _(offset):
        row_spread(col_stat, cs_ss, cs_rs, row_peer(offset)).start()

    @pl.loop(1, n_row)
    def _(offset):
        row_spread_from(col_stat, cs_ss, cs_rs, row_peer(offset)).wait()

    peaks = col_stat[:, 0:1, :]
    top = jnp.max(peaks, axis=0, keepdims=True)
    col_total = jnp.sum(col_stat[:, 1:2, :] * jnp.exp2(peaks - top), axis=0)
    tgt_mass = tgt_mass_ref[...]
    col_pot = log2(tgt_mass) - (top[0] + log2(col_total))
    gain = jnp.exp2(own_peak + col_pot)

    gain_rows = hi_lo_rows(gain)

    def row_sum(block):
        rows = jnp.dot(gain_rows, plan[block], preferred_element_type=jnp.float32)
        return rows[0:1] + rows[1:2]

    @pl.loop(1, n_col)
    def _(offset):
        peer = col_peer(offset)
        sum_send[peer] = row_sum(peer)
        to_owner(sum_send, sum_recv, sum_ss, sum_rs, peer).start()

    sum_recv[me] = row_sum(me)

    @pl.loop(1, n_col)
    def _(offset):
        from_peer(sum_send, sum_recv, sum_ss, sum_rs, col_peer(offset)).wait()

    u_all[me] = own_mass / jnp.sum(sum_recv[...], axis=0)

    @pl.loop(1, n_col)
    def _(offset):
        spread(u_all, u_ss, u_rs, col_peer(offset)).start()

    @pl.loop(1, n_col)
    def _(offset):
        spread_from(u_all, u_ss, u_rs, col_peer(offset)).wait()

    def col_add(block, running):
        return running + lax.dot_general(
            hi_lo_rows(u_all[block]), plan[block], (((1,), (1,)), ((), ())), preferred_element_type=jnp.float32
        )

    both = lax.fori_loop(0, n_col, col_add, jnp.zeros((NUM_ROWS, n_tgt), jnp.float32))
    col_part[mine] = gain * (both[0:1] + both[1:2])

    @pl.loop(1, n_row)
    def _(offset):
        row_spread(col_part, cp_ss, cp_rs, row_peer(offset)).start()

    for block in range(n_col):
        row_out[:, block * width : (block + 1) * width] = POT_SCALE * (rp_all[block] + log2(u_all[block]))

    @pl.loop(1, n_row)
    def _(offset):
        row_spread_from(col_part, cp_ss, cp_rs, row_peer(offset)).wait()

    ratio = tgt_mass / jnp.sum(col_part[...], axis=0)
    col_out[...] = POT_SCALE * (col_pot + log2(ratio))
    factor = gain * ratio
    weighted_high, weighted_low = hi_lo(desc_ref[...].astype(jnp.float32) * factor)
    weights = jnp.concatenate([weighted_high, hi_lo_rows(factor), weighted_low], axis=0)

    def image(block):
        sums = jnp.dot(weights, plan[block], preferred_element_type=jnp.float32)
        den = sums[n_feat : n_feat + 1] + sums[n_feat + 1 : n_feat + 2]
        num = sums[:n_feat] + sums[n_feat + NUM_ROWS :]
        return jnp.concatenate([num.astype(jnp.bfloat16), hi_lo_rows(den)], axis=0)

    @pl.loop(1, n_col)
    def _(offset):
        peer = col_peer(offset)
        num_send[peer] = image(peer)
        to_owner(num_send, num_recv, num_ss, num_rs, peer).start()

    num_recv[me] = image(me)

    @pl.loop(1, n_col)
    def _(offset):
        from_peer(num_send, num_recv, num_ss, num_rs, col_peer(offset)).wait()

    def add(block, running):
        return running + num_recv[block].astype(jnp.float32)

    sums = lax.fori_loop(0, n_col, add, jnp.zeros((n_feat + NUM_ROWS, width), jnp.float32))
    den = sums[n_feat : n_feat + 1] + sums[n_feat + 1 : n_feat + 2]
    map_out[...] = sums[:n_feat] / den


def on_device(n_row, n_col, src_pos, src_desc, src_mass, tgt_pos, tgt_desc, tgt_mass, pattern):
    n_src = src_pos.shape[1]
    n_tgt = tgt_pos.shape[1]
    n_feat = src_desc.shape[0]
    tgt_clusters = n_tgt // CL
    width = n_src // n_col
    column = lax.axis_index("col")
    own = column * tgt_clusters + jnp.arange(tgt_clusters, dtype=jnp.int32)
    named = jnp.any(pattern[None, :, :] == own[:, None, None], axis=2)
    named = jnp.broadcast_to(named[:, :, None], named.shape + (CL,)).reshape(tgt_clusters, n_src)
    n_mask = -(-(4 + tgt_clusters) // 8) * 8 - 4
    src_mask = jnp.where(jnp.pad(named, ((0, n_mask - tgt_clusters), (0, 0)), constant_values=True), 0.0, MASKED)
    depth = n_feat + 6 * (4 + n_mask)

    def blocked(value):
        if width % 128 == 0:
            return value
        return value.reshape(value.shape[0], n_col, width).transpose(1, 0, 2)

    f32, bf16 = jnp.float32, jnp.bfloat16
    vmem = pl.BlockSpec(memory_space=pltpu.VMEM)
    fold = min(width, 128)
    tall = n_feat + NUM_ROWS
    dma = pltpu.SemaphoreType.DMA
    row_pot, col_pot, mapped = pl.pallas_call(
        functools.partial(kernel, n_row, n_col),
        out_shape=(
            jax.ShapeDtypeStruct((1, n_src), f32),
            jax.ShapeDtypeStruct((1, n_tgt), f32),
            jax.ShapeDtypeStruct((n_feat, width), f32),
        ),
        in_specs=[vmem] * 7,
        out_specs=(vmem, vmem, vmem),
        scratch_shapes=[
            pltpu.VMEM((depth, width), bf16),
            pltpu.VMEM((n_tgt, depth), bf16),
            pltpu.VMEM((n_col, n_tgt, width), f32),
            pltpu.VMEM((n_col, n_tgt, width), bf16),
            pltpu.VMEM((n_col, 2, width), f32),
            pltpu.VMEM((n_col, 2, width), f32),
            pltpu.VMEM((n_col, 1, width), f32),
            pltpu.VMEM((n_tgt, fold), f32),
            pltpu.VMEM((n_tgt, fold), f32),
            pltpu.VMEM((n_row, 2, n_tgt), f32),
            pltpu.VMEM((n_col, 1, width), f32),
            pltpu.VMEM((n_col, 1, width), f32),
            pltpu.VMEM((n_col, 1, width), f32),
            pltpu.VMEM((n_row, 1, n_tgt), f32),
            pltpu.VMEM((n_col, tall, width), bf16),
            pltpu.VMEM((n_col, tall, width), bf16),
            dma((n_col,)), dma((n_col,)),
            dma((n_col,)), dma((n_col,)),
            dma((n_row,)), dma((n_row,)),
            dma((n_col,)), dma((n_col,)),
            dma((n_col,)), dma((n_col,)),
            dma((n_row,)), dma((n_row,)),
            dma((n_col,)), dma((n_col,)),
        ],
        compiler_params=pltpu.CompilerParams(
            collective_id=0, has_side_effects=True, vmem_limit_bytes=56 * 1024 * 1024
        ),
    )(
        blocked(src_pos), blocked(src_desc), blocked(src_mask), blocked(src_mass.reshape(1, n_src)),
        tgt_pos, tgt_desc, tgt_mass.reshape(1, n_tgt),
    )
    return (row_pot.reshape(-1), col_pot.reshape(-1), mapped.T)


def solution(mesh):
    in_specs = (
        P(None, "row"),
        P(None, "row"),
        P("row"),
        P(None, "col"),
        P(None, "col"),
        P("col"),
        P("row", None),
    )
    out_specs = (P("row"), P("col"), P(("row", "col"), None))
    body = functools.partial(on_device, mesh.shape["row"], mesh.shape["col"])
    return jax.shard_map(body, mesh=mesh, in_specs=in_specs, out_specs=out_specs, check_vma=False)
```

profile of v0, /device:TPU:13, one launch (start us, length us, event | category | flops | bytes accessed | tf_op | source)
XLA Modules:
  0.0 62.6 jit_solution(14635322201614240315)
XLA Ops:
  0.6 0.8 %compare_reduce_fusion = pred[4,32]{1,0:T(4,128)(4,1)S(1)} fusion(s32[32,20]{0,1:T(8,128)} %param.13, s32[4]{0:T(128)S(1)} %iota_add_fusion), kind=kLoop, calls=%fused_computation.1 | loop fusion | flops 4992 | bytes 2704 | tf_op jit(solution)/shard_map/reduce_or | solution.py:302
  1.5 0.1 broadcast_bitcast_fusion
  1.5 0.7 %copy.13 = f32[1,4,32,128]{3,1,2,0:T(4,128)} copy(f32[1,4,32,128]{3,2,1,0:T(8,128)S(1)} %broadcast_bitcast_fusion) | data formatting | bytes 131072
  2.2 56.9 %shard_map.94 = (f32[1,4096]{1,0:T(1,128)}, f32[1,512]{1,0:T(1,128)}, f32[64,256]{1,0:T(8,128)}) custom-call(f32[3,4096]{1,0:T(4,128)} %src_pos_ref.1, bf16[64,4096]{1,0:T(8,128)(2,1)} %src_desc_ref.1, f32[4,4096]{1,0:T(4,128)} %bitcast.10, f32[1,4096]{1,0:T(1,128)} %bitcast.12, f32[3,512]{1,0:T(4,128)} %tgt_pos_ref.1, bf16[64,512]{1,0:T(8,128)(2,1)} %desc_ref.1, ...), custom_call_target="tpu_custom_call" | custom-call | tf_op jit(solution)/shard_map/pallas_call | solution.py:318
  59.2 0.0 copy-start
  59.2 1.3 %copy.17 = f32[4096]{0:T(1024)} copy(f32[4096]{0:T(1024)} %bitcast.13) | data formatting | bytes 32768
  60.5 0.0 copy-done
  60.5 0.6 copy.18
  61.1 1.5 %copy.19 = f32[256,64]{0,1:T(8,128)} copy(f32[256,64]{0,1:T(8,128)} %bitcast.11) | data formatting | bytes 131072
  (2 shorter events, 0.0 us)
Async XLA Ops:
  59.2 1.3 %copy-start = (f32[1,512]{1,0:T(1,128)S(1)}, f32[1,512]{1,0:T(1,128)}, u32[]{:S(2)}) copy-start(f32[1,512]{1,0:T(1,128)} %get-tuple-element.7) | copy-start | bytes 6148
where the time goes:
time: 62.9 us; the launch traced here: 62.6 us
  Pallas kernels  56.9 us (90%)
  local copies, waits for them, and re-layouts  4.14 us (7%)
  other arithmetic  0.82 us (1%)
  between operations  0.66 us (1%)
    pallas_call x1, Pallas kernels, on_device(): pl.pallas_call(functools.partial(kernel, n_row, n_col), out_shape=(jax.Sh...  56.9 us
    unnamed x7, local copies, waits for them, and re-layouts  4.14 us

commit v1 on v0

--- a/solution.py
+++ b/solution.py
@@ -43,13 +43,21 @@
     return rows.astype(jnp.bfloat16)
 
 
+def flipped(place, mask, count):
+    bits = count.bit_length() - 1
+    if count != 1 << bits:
+        return lax.rem(place + mask, count)
+    digits = [lax.rem(lax.div(place, 1 << bit) + lax.div(mask, 1 << bit), 2) for bit in range(bits)]
+    return sum(digit * (1 << bit) for bit, digit in enumerate(digits))
+
+
 def kernel(
     n_row, n_col,
     src_pos_ref, src_desc_ref, src_mask_ref, src_mass_ref, tgt_pos_ref, desc_ref, tgt_mass_ref,
     row_out, col_out, map_out,
     src_feat, tgt_feat, score, plan, stat_send, stat_recv, rp_all, col_max, col_sum, col_stat, sum_send, sum_recv, u_all,
-    col_part, num_send, num_recv,
-    stat_ss, stat_rs, rp_ss, rp_rs, cs_ss, cs_rs, sum_ss, sum_rs, u_ss, u_rs, cp_ss, cp_rs, num_ss, num_rs,
+    col_part, pair_send, pair_recv, num_send, num_recv, den_send, den_recv,
+    stat_ss, stat_rs, rp_ss, rp_rs, cs_ss, cs_rs, sum_ss, sum_rs, u_ss, u_rs, cp_ss, cp_rs, pair_ss, pair_rs, num_ss, num_rs, den_ss, den_rs,
 ):
     me = lax.axis_index("col")
     mine = lax.axis_index("row")
@@ -59,7 +67,7 @@
     n_feat = desc_ref.shape[0]
 
     def col_peer(offset):
-        return lax.rem(me + offset, n_col)
+        return flipped(me, n_col - offset, n_col)
 
     def row_peer(offset):
         return lax.rem(mine + offset, n_row)
@@ -141,9 +149,22 @@
     peak, total = row_stat(me)
     stat_recv[me, 0:1, :] = peak
     stat_recv[me, 1:2, :] = total
+    early = n_col // 2
+
+    @pl.loop(1, early)
+    def _(offset):
+        peer = col_peer(offset)
+        peak, total = row_stat(peer)
+        stat_send[peer, 0:1, :] = peak
+        stat_send[peer, 1:2, :] = total
+
     pl.semaphore_wait(barrier, n_col - 1 + n_row - 1)
 
-    @pl.loop(1, n_col)
+    @pl.loop(1, early)
+    def _(offset):
+        to_owner(stat_send, stat_recv, stat_ss, stat_rs, col_peer(offset)).start()
+
+    @pl.loop(early, n_col)
     def _(offset):
         peer = col_peer(offset)
         peak, total = row_stat(peer)
@@ -265,30 +286,75 @@
     weighted_high, weighted_low = hi_lo(desc_ref[...].astype(jnp.float32) * factor)
     weights = jnp.concatenate([weighted_high, hi_lo_rows(factor), weighted_low], axis=0)
 
+    n_chip = n_col // 2
+    chip = me // 2
+    core = lax.rem(me, 2)
+
     def image(block):
         sums = jnp.dot(weights, plan[block], preferred_element_type=jnp.float32)
         den = sums[n_feat : n_feat + 1] + sums[n_feat + 1 : n_feat + 2]
-        num = sums[:n_feat] + sums[n_feat + NUM_ROWS :]
-        return jnp.concatenate([num.astype(jnp.bfloat16), hi_lo_rows(den)], axis=0)
-
-    @pl.loop(1, n_col)
-    def _(offset):
-        peer = col_peer(offset)
-        num_send[peer] = image(peer)
-        to_owner(num_send, num_recv, num_ss, num_rs, peer).start()
-
-    num_recv[me] = image(me)
-
-    @pl.loop(1, n_col)
-    def _(offset):
-        from_peer(num_send, num_recv, num_ss, num_rs, col_peer(offset)).wait()
-
-    def add(block, running):
-        return running + num_recv[block].astype(jnp.float32)
-
-    sums = lax.fori_loop(0, n_col, add, jnp.zeros((n_feat + NUM_ROWS, width), jnp.float32))
-    den = sums[n_feat : n_feat + 1] + sums[n_feat + 1 : n_feat + 2]
-    map_out[...] = sums[:n_feat] / den
+        return sums[:n_feat] + sums[n_feat + NUM_ROWS :], den
+
+    def to_pair(place):
+        return pltpu.make_async_remote_copy(
+            src_ref=pair_send.at[place], dst_ref=pair_recv.at[place],
+            send_sem=pair_ss.at[place], recv_sem=pair_rs.at[place],
+            device_id={"col": 2 * chip + 1 - core}, device_id_type=MESH,
+        )
+
+    def to_image(send, recv, ssem, rsem, place):
+        return pltpu.make_async_remote_copy(
+            src_ref=send.at[place], dst_ref=recv.at[chip], send_sem=ssem.at[place], recv_sem=rsem.at[chip],
+            device_id={"col": 2 * place + core}, device_id_type=MESH,
+        )
+
+    def from_image(send, recv, ssem, rsem, place):
+        return pltpu.make_async_remote_copy(
+            src_ref=send.at[place], dst_ref=recv.at[place], send_sem=ssem.at[place], recv_sem=rsem.at[place],
+            device_id={"col": 2 * place + core}, device_id_type=MESH,
+        )
+
+    def chip_peer(offset):
+        return flipped(chip, n_chip - offset, n_chip)
+
+    def pair_start(place):
+        num, den = image(2 * place + 1 - core)
+        pair_send[place, 0:n_feat, :] = num
+        pair_send[place, n_feat:, :] = jnp.broadcast_to(den, (8, width))
+        to_pair(place).start()
+
+    @pl.loop(1, n_chip)
+    def _(offset):
+        pair_start(chip_peer(offset))
+
+    pair_start(chip)
+
+    def pair_total(place):
+        num, den = image(2 * place + core)
+        to_pair(place).wait()
+        return num + pair_recv[place, 0:n_feat, :], den + pair_recv[place, n_feat : n_feat + 1, :]
+
+    @pl.loop(1, n_chip)
+    def _(offset):
+        place = chip_peer(offset)
+        num, den = pair_total(place)
+        num_send[place] = num.astype(jnp.bfloat16)
+        den_send[place] = den
+        to_image(num_send, num_recv, num_ss, num_rs, place).start()
+        to_image(den_send, den_recv, den_ss, den_rs, place).start()
+
+    num, den = pair_total(chip)
+    map_out[...] = num
+    den_recv[chip] = den
+
+    @pl.loop(1, n_chip)
+    def _(offset):
+        place = chip_peer(offset)
+        from_image(num_send, num_recv, num_ss, num_rs, place).wait()
+        from_image(den_send, den_recv, den_ss, den_rs, place).wait()
+        map_out[...] += num_recv[place].astype(jnp.float32)
+
+    map_out[...] = map_out[...] / jnp.sum(den_recv[...], axis=0)
 
 
 def on_device(n_row, n_col, src_pos, src_desc, src_mass, tgt_pos, tgt_desc, tgt_mass, pattern):
@@ -313,7 +379,6 @@
     f32, bf16 = jnp.float32, jnp.bfloat16
     vmem = pl.BlockSpec(memory_space=pltpu.VMEM)
     fold = min(width, 128)
-    tall = n_feat + NUM_ROWS
     dma = pltpu.SemaphoreType.DMA
     row_pot, col_pot, mapped = pl.pallas_call(
         functools.partial(kernel, n_row, n_col),
@@ -339,15 +404,21 @@
             pltpu.VMEM((n_col, 1, width), f32),
             pltpu.VMEM((n_col, 1, width), f32),
             pltpu.VMEM((n_row, 1, n_tgt), f32),
-            pltpu.VMEM((n_col, tall, width), bf16),
-            pltpu.VMEM((n_col, tall, width), bf16),
+            pltpu.VMEM((n_col // 2, n_feat + 8, width), f32),
+            pltpu.VMEM((n_col // 2, n_feat + 8, width), f32),
+            pltpu.VMEM((n_col // 2, n_feat, width), bf16),
+            pltpu.VMEM((n_col // 2, n_feat, width), bf16),
+            pltpu.VMEM((n_col // 2, 1, width), f32),
+            pltpu.VMEM((n_col // 2, 1, width), f32),
             dma((n_col,)), dma((n_col,)),
             dma((n_col,)), dma((n_col,)),
             dma((n_row,)), dma((n_row,)),
             dma((n_col,)), dma((n_col,)),
             dma((n_col,)), dma((n_col,)),
             dma((n_row,)), dma((n_row,)),
-            dma((n_col,)), dma((n_col,)),
+            dma((n_col // 2,)), dma((n_col // 2,)),
+            dma((n_col // 2,)), dma((n_col // 2,)),
+            dma((n_col // 2,)), dma((n_col // 2,)),
         ],
         compiler_params=pltpu.CompilerParams(
             collective_id=0, has_side_effects=True, vmem_limit_bytes=56 * 1024 * 1024

time: 62.9 us -> 54.9 us (0.87)
  the two profiles are of different devices: /device:TPU:13 before, /device:TPU:0 now
where the time goes in v1:
time: 54.9 us; the launch traced here: 54.6 us
  Pallas kernels  49 us (89%)
  local copies, waits for them, and re-layouts  4.14 us (8%)
  other arithmetic  0.82 us (1%)
  between operations  0.66 us (1%)
    pallas_call x1, Pallas kernels, on_device(): pl.pallas_call(functools.partial(kernel, n_row, n_col), out_shape=(jax.Sh...  49 us
    unnamed x7, local copies, waits for them, and re-layouts  4.14 us

profile of v1, /device:TPU:0, one launch (start us, length us, event | category | flops | bytes accessed | tf_op | source)
XLA Modules:
  0.0 54.6 jit_solution(17033970313511695306)
XLA Ops:
  0.6 0.8 %compare_reduce_fusion = pred[4,32]{1,0:T(4,128)(4,1)S(1)} fusion(s32[32,20]{0,1:T(8,128)} %param.13, s32[4]{0:T(128)S(1)} %iota_add_fusion), kind=kLoop, calls=%fused_computation.1 | loop fusion | flops 4992 | bytes 2704 | tf_op jit(solution)/shard_map/reduce_or | solution.py:368
  1.5 0.1 broadcast_bitcast_fusion
  1.5 0.7 %copy.13 = f32[1,4,32,128]{3,1,2,0:T(4,128)} copy(f32[1,4,32,128]{3,2,1,0:T(8,128)S(1)} %broadcast_bitcast_fusion) | data formatting | bytes 131072
  2.2 49.0 %shard_map.94 = (f32[1,4096]{1,0:T(1,128)}, f32[1,512]{1,0:T(1,128)}, f32[64,256]{1,0:T(8,128)}) custom-call(f32[3,4096]{1,0:T(4,128)} %src_pos_ref.1, bf16[64,4096]{1,0:T(8,128)(2,1)} %src_desc_ref.1, f32[4,4096]{1,0:T(4,128)} %bitcast.10, f32[1,4096]{1,0:T(1,128)} %bitcast.12, f32[3,512]{1,0:T(4,128)} %tgt_pos_ref.1, bf16[64,512]{1,0:T(8,128)(2,1)} %desc_ref.1, ...), custom_call_target="tpu_custom_call" | custom-call | tf_op jit(solution)/shard_map/pallas_call | solution.py:383
  51.2 0.0 copy-start
  51.2 1.3 %copy.17 = f32[4096]{0:T(1024)} copy(f32[4096]{0:T(1024)} %bitcast.13) | data formatting | bytes 32768
  52.6 0.0 copy-done
  52.6 0.6 %copy.18 = f32[512]{0:T(512)} copy(f32[512]{0:T(512)S(1)} %bitcast.15) | data formatting | bytes 4096
  53.1 1.5 %copy.19 = f32[256,64]{0,1:T(8,128)} copy(f32[256,64]{0,1:T(8,128)} %bitcast.11) | data formatting | bytes 131072
  (2 shorter events, 0.0 us)
Async XLA Ops:
  51.2 1.3 %copy-start = (f32[1,512]{1,0:T(1,128)S(1)}, f32[1,512]{1,0:T(1,128)}, u32[]{:S(2)}) copy-start(f32[1,512]{1,0:T(1,128)} %get-tuple-element.7) | copy-start | bytes 6148

commit v2 on v1

--- a/solution.py
+++ b/solution.py
@@ -53,7 +53,7 @@
 
 def kernel(
     n_row, n_col,
-    src_pos_ref, src_desc_ref, src_mask_ref, src_mass_ref, tgt_pos_ref, desc_ref, tgt_mass_ref,
+    src_pos_ref, src_desc_ref, pattern_ref, src_mass_ref, tgt_pos_ref, desc_ref, tgt_mass_ref,
     row_out, col_out, map_out,
     src_feat, tgt_feat, score, plan, stat_send, stat_recv, rp_all, col_max, col_sum, col_stat, sum_send, sum_recv, u_all,
     col_part, pair_send, pair_recv, num_send, num_recv, den_send, den_recv,
@@ -126,19 +126,27 @@
     desc32 = desc_ref[...].astype(jnp.float32)
     tgt_pos = tgt_pos_ref[...]
     norm = jnp.sum(tgt_pos * tgt_pos, axis=0, keepdims=True) + jnp.sum(desc32 * desc32, axis=0, keepdims=True)
-    n_mask = src_mask_ref.shape[-2]
-    lane = lax.broadcasted_iota(jnp.int32, (n_mask, n_tgt), 1) // CL
-    in_cluster = lane == lax.broadcasted_iota(jnp.int32, (n_mask, n_tgt), 0)
-    t1, t2, t3 = float_parts(jnp.concatenate([tgt_pos, -0.5 * norm, jnp.where(in_cluster, 1.0, 0.0)], axis=0))
-    tgt_feat[...] = jnp.concatenate([desc32, t1, t2, t1, t2, t3, t1], axis=0).T.astype(jnp.bfloat16)
+    t1, t2, t3 = float_parts(jnp.concatenate([tgt_pos, -0.5 * norm], axis=0))
+    upper = n_feat + 24
+    tgt_feat[:, 0:upper] = jnp.concatenate([desc32, t1, t2, t1, t2, t3, t1], axis=0).T.astype(jnp.bfloat16)
+    pattern = pattern_ref[...]
+    n_cluster = pattern.shape[1]
+    for place in range(n_tgt // CL):
+        hits = jnp.where(pattern == me * (n_tgt // CL) + place, 1.0, 0.0)
+        mask = jnp.where(jnp.max(hits, axis=0, keepdims=True) > 0.5, 0.0, MASKED)
+        tgt_feat[place * CL : (place + 1) * CL, upper:] = jnp.broadcast_to(mask, (CL, n_cluster)).astype(jnp.bfloat16)
+    source = lax.broadcasted_iota(jnp.int32, (n_cluster, width), 1)
+    cluster = lax.broadcasted_iota(jnp.int32, (n_cluster, width), 0) * CL
     ones = jnp.ones((1, width), jnp.float32)
 
     def row_stat(block):
         s1, s2, s3 = float_parts(
-            jnp.concatenate([block_of(src_pos_ref, block), ones, block_of(src_mask_ref, block)], axis=0)
-        )
+            jnp.concatenate([block_of(src_pos_ref, block), ones], axis=0)
+        )
+        past = source + block * width - cluster
+        in_cluster = jnp.where((past >= 0) & (past < CL), 1.0, 0.0)
         src_feat[0:n_feat, :] = block_of(src_desc_ref, block)
-        src_feat[n_feat:, :] = jnp.concatenate([s1, s1, s2, s2, s1, s3], axis=0).astype(jnp.bfloat16)
+        src_feat[n_feat:, :] = jnp.concatenate([s1, s1, s2, s2, s1, s3, in_cluster], axis=0).astype(jnp.bfloat16)
         score[block] = SCORE_SCALE * jnp.dot(
             tgt_feat[...], src_feat[...], preferred_element_type=jnp.float32
         )
@@ -357,19 +365,18 @@
     map_out[...] = map_out[...] / jnp.sum(den_recv[...], axis=0)
 
 
+def hand_out(row_in, col_in, map_in, row_out, col_out, map_out):
+    row_out[...] = row_in[...]
+    col_out[...] = col_in[...]
+    map_out[...] = map_in[...]
+
+
 def on_device(n_row, n_col, src_pos, src_desc, src_mass, tgt_pos, tgt_desc, tgt_mass, pattern):
     n_src = src_pos.shape[1]
     n_tgt = tgt_pos.shape[1]
     n_feat = src_desc.shape[0]
-    tgt_clusters = n_tgt // CL
     width = n_src // n_col
-    column = lax.axis_index("col")
-    own = column * tgt_clusters + jnp.arange(tgt_clusters, dtype=jnp.int32)
-    named = jnp.any(pattern[None, :, :] == own[:, None, None], axis=2)
-    named = jnp.broadcast_to(named[:, :, None], named.shape + (CL,)).reshape(tgt_clusters, n_src)
-    n_mask = -(-(4 + tgt_clusters) // 8) * 8 - 4
-    src_mask = jnp.where(jnp.pad(named, ((0, n_mask - tgt_clusters), (0, 0)), constant_values=True), 0.0, MASKED)
-    depth = n_feat + 6 * (4 + n_mask)
+    depth = n_feat + 24 + pattern.shape[0]
 
     def blocked(value):
         if width % 128 == 0:
@@ -424,9 +431,16 @@
             collective_id=0, has_side_effects=True, vmem_limit_bytes=56 * 1024 * 1024
         ),
     )(
-        blocked(src_pos), blocked(src_desc), blocked(src_mask), blocked(src_mass.reshape(1, n_src)),
+        blocked(src_pos), blocked(src_desc), pattern.T, blocked(src_mass.reshape(1, n_src)),
         tgt_pos, tgt_desc, tgt_mass.reshape(1, n_tgt),
     )
+    row_pot, col_pot, mapped = pl.pallas_call(
+        hand_out,
+        out_shape=tuple(jax.ShapeDtypeStruct(value.shape, f32) for value in (row_pot, col_pot, mapped)),
+        in_specs=[vmem] * 3,
+        out_specs=(vmem, vmem, vmem),
+        compiler_params=pltpu.CompilerParams(vmem_limit_bytes=4 * 1024 * 1024),
+    )(row_pot, col_pot, mapped)
     return (row_pot.reshape(-1), col_pot.reshape(-1), mapped.T)
 
 

time: 54.9 us -> 52.8 us (0.962)
  local copies, waits for them, and re-layouts: 4.14 us -> 2.2 us
  other arithmetic: 0.82 us -> 0 us
  Pallas kernels: 49 us -> 49.7 us
    unnamed x7 -> x6, local copies, waits for them, and re-layouts: 4.14 us -> 2.2 us
    reduce_or x1 -> x0, other arithmetic: 0.81 us -> none  [on_device(): named = jnp.any(pattern[None, :, :] == own[:, None, None], axis=2)]
    pallas_call x0 -> x1, Pallas kernels: none -> 0.64 us  [on_device(): pl.pallas_call(hand_out, out_shape=tuple((jax.ShapeDtypeStruct(value.shap...]
where the time goes in v2:
time: 52.8 us; the launch traced here: 52.5 us
  Pallas kernels  49.7 us (94%)
  local copies, waits for them, and re-layouts  2.2 us (4%)
  between operations  0.65 us (1%)
    pallas_call x1, Pallas kernels, on_device(): pl.pallas_call(functools.partial(kernel, n_row, n_col), out_shape=(jax.Sh...  49 us
    unnamed x6, local copies, waits for them, and re-layouts  2.2 us

profile of v2, /device:TPU:0, one launch (start us, length us, event | category | flops | bytes accessed | tf_op | source)
XLA Modules:
  0.0 52.5 jit_solution(1128190244761216891)
XLA Ops:
  0.6 49.0 %shard_map.94 = (f32[1,4096]{1,0:T(1,128)}, f32[1,512]{1,0:T(1,128)}, f32[64,256]{1,0:T(8,128)}) custom-call(f32[3,4096]{1,0:T(4,128)} %src_pos_ref.1, bf16[64,4096]{1,0:T(8,128)(2,1)} %src_desc_ref.1, s32[20,32]{1,0:T(8,128)} %bitcast.7, f32[1,4096]{1,0:T(1,128)} %bitcast.6, f32[3,512]{1,0:T(4,128)} %tgt_pos_ref.1, bf16[64,512]{1,0:T(8,128)(2,1)} %desc_ref.1, ...), custom_call_target="tpu_custom_call" | custom-call | tf_op jit(solution)/shard_map/pallas_call | solution.py:390
  49.7 0.0 copy-start.2
  49.7 0.6 %copy-done.2 = f32[1,512]{1,0:T(1,128)S(1)} copy-done((f32[1,512]{1,0:T(1,128)S(1)}, f32[1,512]{1,0:T(1,128)}, u32[]{:S(2)}) %copy-start.2) | copy-done | bytes 2072
  50.3 0.0 copy-start
  50.3 0.8 %copy-done = f32[64,256]{1,0:T(8,128)S(1)} copy-done((f32[64,256]{1,0:T(8,128)S(1)}, f32[64,256]{1,0:T(8,128)}, u32[]{:S(2)}) %copy-start) | copy-done | bytes 65560
  51.2 0.0 copy-start.1
  51.2 0.7 %copy-done.1 = f32[1,4096]{1,0:T(1,128)S(1)} copy-done((f32[1,4096]{1,0:T(1,128)S(1)}, f32[1,4096]{1,0:T(1,128)}, u32[]{:S(2)}) %copy-start.1) | copy-done | bytes 16408
  51.9 0.6 %shard_map.95 = (f32[1,4096]{1,0:T(1,128)}, f32[1,512]{1,0:T(1,128)}, f32[64,256]{1,0:T(8,128)}) custom-call(f32[1,4096]{1,0:T(1,128)S(1)} %copy-done.1, f32[1,512]{1,0:T(1,128)S(1)} %copy-done.2, f32[64,256]{1,0:T(8,128)S(1)} %copy-done), custom_call_target="tpu_custom_call" | custom-call | tf_op jit(solution)/shard_map/pallas_call | solution.py:437
Async XLA Ops:
  49.7 0.7 %copy-start.2 = (f32[1,512]{1,0:T(1,128)S(1)}, f32[1,512]{1,0:T(1,128)}, u32[]{:S(2)}) copy-start(f32[1,512]{1,0:T(1,128)} %get-tuple-element.10.col_in) | copy-start | bytes 6148
  50.3 0.8 %copy-start = (f32[64,256]{1,0:T(8,128)S(1)}, f32[64,256]{1,0:T(8,128)}, u32[]{:S(2)}) copy-start(f32[64,256]{1,0:T(8,128)} %get-tuple-element.11.map_in) | copy-start | bytes 196612
  51.2 0.7 %copy-start.1 = (f32[1,4096]{1,0:T(1,128)S(1)}, f32[1,4096]{1,0:T(1,128)}, u32[]{:S(2)}) copy-start(f32[1,4096]{1,0:T(1,128)} %get-tuple-element.9.row_in) | copy-start | bytes 49156

commit v3 on v2

--- a/solution.py
+++ b/solution.py
@@ -84,27 +84,22 @@
 
     def to_owner(send, recv, ssem, rsem, peer):
         return pltpu.make_async_remote_copy(
-            src_ref=send.at[peer], dst_ref=recv.at[me], send_sem=ssem.at[peer], recv_sem=rsem.at[me],
+            src_ref=send.at[peer], dst_ref=recv.at[me], send_sem=ssem.at[0], recv_sem=rsem.at[0],
             device_id={"col": peer}, device_id_type=MESH,
         )
 
-    def from_peer(send, recv, ssem, rsem, peer):
-        return pltpu.make_async_remote_copy(
-            src_ref=send.at[peer], dst_ref=recv.at[peer], send_sem=ssem.at[peer], recv_sem=rsem.at[peer],
+    def spread(buf, ssem, rsem, peer):
+        return pltpu.make_async_remote_copy(
+            src_ref=buf.at[me], dst_ref=buf.at[me], send_sem=ssem.at[0], recv_sem=rsem.at[0],
             device_id={"col": peer}, device_id_type=MESH,
         )
 
-    def spread(buf, ssem, rsem, peer):
-        return pltpu.make_async_remote_copy(
-            src_ref=buf.at[me], dst_ref=buf.at[me], send_sem=ssem.at[peer], recv_sem=rsem.at[me],
-            device_id={"col": peer}, device_id_type=MESH,
-        )
-
-    def spread_from(buf, ssem, rsem, peer):
-        return pltpu.make_async_remote_copy(
-            src_ref=buf.at[me], dst_ref=buf.at[peer], send_sem=ssem.at[peer], recv_sem=rsem.at[peer],
-            device_id={"col": peer}, device_id_type=MESH,
-        )
+    def wait_all(send, recv, ssem, rsem):
+        pltpu.make_async_remote_copy(
+            src_ref=send.at[pl.ds(0, n_col - 1)], dst_ref=recv.at[pl.ds(0, n_col - 1)],
+            send_sem=ssem.at[0], recv_sem=rsem.at[0],
+            device_id={"col": lax.rem(me + 1, n_col)}, device_id_type=MESH,
+        ).wait()
 
     def row_spread(buf, ssem, rsem, peer):
         return pltpu.make_async_remote_copy(
@@ -180,9 +175,7 @@
         stat_send[peer, 1:2, :] = total
         to_owner(stat_send, stat_recv, stat_ss, stat_rs, peer).start()
 
-    @pl.loop(1, n_col)
-    def _(offset):
-        from_peer(stat_send, stat_recv, stat_ss, stat_rs, col_peer(offset)).wait()
+    wait_all(stat_send, stat_recv, stat_ss, stat_rs)
 
     peaks = stat_recv[:, 0:1, :]
     top = jnp.max(peaks, axis=0, keepdims=True)
@@ -194,9 +187,7 @@
     def _(offset):
         spread(rp_all, rp_ss, rp_rs, col_peer(offset)).start()
 
-    @pl.loop(1, n_col)
-    def _(offset):
-        spread_from(rp_all, rp_ss, rp_rs, col_peer(offset)).wait()
+    wait_all(rp_all, rp_all, rp_ss, rp_rs)
 
     strip = 64
 
@@ -255,19 +246,15 @@
 
     sum_recv[me] = row_sum(me)
 
+    wait_all(sum_send, sum_recv, sum_ss, sum_rs)
+
+    u_all[me] = own_mass / jnp.sum(sum_recv[...], axis=0)
+
     @pl.loop(1, n_col)
     def _(offset):
-        from_peer(sum_send, sum_recv, sum_ss, sum_rs, col_peer(offset)).wait()
-
-    u_all[me] = own_mass / jnp.sum(sum_recv[...], axis=0)
-
-    @pl.loop(1, n_col)
-    def _(offset):
         spread(u_all, u_ss, u_rs, col_peer(offset)).start()
 
-    @pl.loop(1, n_col)
-    def _(offset):
-        spread_from(u_all, u_ss, u_rs, col_peer(offset)).wait()
+    wait_all(u_all, u_all, u_ss, u_rs)
 
     def col_add(block, running):
         return running + lax.dot_general(
@@ -417,11 +404,11 @@
             pltpu.VMEM((n_col // 2, n_feat, width), bf16),
             pltpu.VMEM((n_col // 2, 1, width), f32),
             pltpu.VMEM((n_col // 2, 1, width), f32),
-            dma((n_col,)), dma((n_col,)),
-            dma((n_col,)), dma((n_col,)),
+            dma((1,)), dma((1,)),
+            dma((1,)), dma((1,)),
             dma((n_row,)), dma((n_row,)),
-            dma((n_col,)), dma((n_col,)),
-            dma((n_col,)), dma((n_col,)),
+            dma((1,)), dma((1,)),
+            dma((1,)), dma((1,)),
             dma((n_row,)), dma((n_row,)),
             dma((n_col // 2,)), dma((n_col // 2,)),
             dma((n_col // 2,)), dma((n_col // 2,)),

time: 52.8 us -> 51.4 us (0.973)
  Pallas kernels: 49.7 us -> 48.3 us
    pallas_call x1, Pallas kernels: 49 us -> 47.6 us  [on_device(): pl.pallas_call(functools.partial(kernel, n_row, n_col), out_shape=(jax.Sh...]
where the time goes in v3:
time: 51.4 us; the launch traced here: 51.1 us
  Pallas kernels  48.3 us (94%)
  local copies, waits for them, and re-layouts  2.2 us (4%)
  between operations  0.65 us (1%)
    pallas_call x1, Pallas kernels, on_device(): pl.pallas_call(functools.partial(kernel, n_row, n_col), out_shape=(jax.Sh...  47.6 us
    unnamed x6, local copies, waits for them, and re-layouts  2.2 us

profile of v3, /device:TPU:0, one launch (start us, length us, event | category | flops | bytes accessed | tf_op | source)
XLA Modules:
  0.0 51.1 jit_solution(4289815535040223487)
XLA Ops:
  0.6 47.6 %shard_map.94 = (f32[1,4096]{1,0:T(1,128)}, f32[1,512]{1,0:T(1,128)}, f32[64,256]{1,0:T(8,128)}) custom-call(f32[3,4096]{1,0:T(4,128)} %src_pos_ref.1, bf16[64,4096]{1,0:T(8,128)(2,1)} %src_desc_ref.1, s32[20,32]{1,0:T(8,128)} %bitcast.7, f32[1,4096]{1,0:T(1,128)} %bitcast.6, f32[3,512]{1,0:T(4,128)} %tgt_pos_ref.1, bf16[64,512]{1,0:T(8,128)(2,1)} %desc_ref.1, ...), custom_call_target="tpu_custom_call" | custom-call | tf_op jit(solution)/shard_map/pallas_call | solution.py:377
  48.3 0.0 copy-start.2
  48.3 0.6 %copy-done.2 = f32[1,512]{1,0:T(1,128)S(1)} copy-done((f32[1,512]{1,0:T(1,128)S(1)}, f32[1,512]{1,0:T(1,128)}, u32[]{:S(2)}) %copy-start.2) | copy-done | bytes 2072
  48.9 0.0 copy-start
  48.9 0.8 %copy-done = f32[64,256]{1,0:T(8,128)S(1)} copy-done((f32[64,256]{1,0:T(8,128)S(1)}, f32[64,256]{1,0:T(8,128)}, u32[]{:S(2)}) %copy-start) | copy-done | bytes 65560
  49.8 0.0 copy-start.1
  49.8 0.7 %copy-done.1 = f32[1,4096]{1,0:T(1,128)S(1)} copy-done((f32[1,4096]{1,0:T(1,128)S(1)}, f32[1,4096]{1,0:T(1,128)}, u32[]{:S(2)}) %copy-start.1) | copy-done | bytes 16408
  50.5 0.6 %shard_map.95 = (f32[1,4096]{1,0:T(1,128)}, f32[1,512]{1,0:T(1,128)}, f32[64,256]{1,0:T(8,128)}) custom-call(f32[1,4096]{1,0:T(1,128)S(1)} %copy-done.1, f32[1,512]{1,0:T(1,128)S(1)} %copy-done.2, f32[64,256]{1,0:T(8,128)S(1)} %copy-done), custom_call_target="tpu_custom_call" | custom-call | tf_op jit(solution)/shard_map/pallas_call | solution.py:424
Async XLA Ops:
  48.3 0.7 %copy-start.2 = (f32[1,512]{1,0:T(1,128)S(1)}, f32[1,512]{1,0:T(1,128)}, u32[]{:S(2)}) copy-start(f32[1,512]{1,0:T(1,128)} %get-tuple-element.10.col_in) | copy-start | bytes 6148
  48.9 0.8 %copy-start = (f32[64,256]{1,0:T(8,128)S(1)}, f32[64,256]{1,0:T(8,128)}, u32[]{:S(2)}) copy-start(f32[64,256]{1,0:T(8,128)} %get-tuple-element.11.map_in) | copy-start | bytes 196612
  49.8 0.7 %copy-start.1 = (f32[1,4096]{1,0:T(1,128)S(1)}, f32[1,4096]{1,0:T(1,128)}, u32[]{:S(2)}) copy-start(f32[1,4096]{1,0:T(1,128)} %get-tuple-element.9.row_in) | copy-start | bytes 49156
